TPU v7x, 512 devices: a whole 4x8x8 slice. The times are simulated.
512 devices in a mesh: row: 32 (over y, x), col: 16 (over z, core).
Axes of the slice: x: 4, y: 8, z: 8, core: 2. Of those that a mesh axis runs over, the one named last changes fastest.
Arguments:
- kernel_matrix: float32 [16384, 16384], P('row', 'col'), may hold values from 0 to 2, as said below
Outputs:
- factored: float32 [16384, 16384], P('row', 'col')
Inputs may be any that keep to these rules, and one draw needn't show every extreme that they name: kernel_matrix, put in global order by the element-cyclic map, is symmetric: a Gaussian-process kernel amp * exp(-distance / scale) over random points plus a nugget of at least 0.5 on the diagonal, so it is positive definite with smallest eigenvalue at least 0.5.
All inputs are finite; a program needn't handle non-finite values.
Results may differ from a plain program's by a relative error of at most 0.00025.
Values sent between devices are 32-bit elements; how exact they have to be, the bound alone decides.
No kernel may reach another device: no remote copies, remote signals or barrier semaphores. Data moves between devices by JAX's collectives and lax.ppermute only.
A program may use at most 64 MiB of HBM per device.

v0:
```python
import jax
import jax.numpy as jnp
from jax import lax
from jax.sharding import PartitionSpec as P

PANEL = 192
PANELS = 2


def spread(block, axis, source):
    block = jnp.where(lax.axis_index(axis) == source, block, jnp.zeros_like(block))
    return lax.psum(block, axis)


def solve_rows(lower_factor, rows):
    return lax.linalg.triangular_solve(
        lower_factor, rows, left_side=False, lower=True, transpose_a=True
    )


def alternate_cols(block, groups):
    height = block.shape[0]
    inner = block.shape[1] // groups
    return block.reshape(height, groups, inner).transpose(0, 2, 1).reshape(height, groups * inner)


def alternate_rows(block, groups):
    inner = block.shape[0] // groups
    breadth = block.shape[1]
    return block.reshape(groups, inner, breadth).transpose(1, 0, 2).reshape(groups * inner, breadth)


def per_device(kernel_matrix):
    matrix = kernel_matrix
    row_count = lax.axis_size("row")
    col_count = lax.axis_size("col")
    row_share = row_count // col_count
    local_rows, local_cols = matrix.shape
    tile_rows = PANEL // row_count
    tile_cols = PANEL // col_count
    col_index = lax.axis_index("col")
    for current in range(PANELS):
        factor_row_start = current * tile_rows
        factor_col_start = current * tile_cols
        factor_col_rest = factor_col_start + tile_cols
        corner = matrix[
            factor_row_start : factor_row_start + tile_rows, factor_col_start:factor_col_rest
        ]
        corner = lax.all_gather(corner, "row", axis=0, tiled=True)
        corner = lax.all_gather(corner, "col", axis=1, tiled=True)
        corner = alternate_cols(alternate_rows(corner, row_count), col_count)
        lower_factor = jnp.linalg.cholesky(corner)
        column_block = matrix[:, factor_col_start:factor_col_rest]
        gathered = alternate_cols(
            lax.all_gather(column_block, "col", axis=1, tiled=True), col_count
        )
        factor_left_rows = solve_rows(lower_factor, gathered)
        received = []
        for source in range(row_share):
            received.append(spread(factor_left_rows, "row", col_index + source * col_count))
        factor_right_rows = jnp.stack(received, axis=1).reshape(local_cols, PANEL)[factor_col_rest:]
        row_start = current * tile_rows
        col_start = current * tile_cols
        owned = factor_left_rows.reshape(local_rows, tile_cols, col_count)
        owned = lax.dynamic_index_in_dim(owned, col_index, axis=2, keepdims=False)
        matrix = matrix.at[row_start:, col_start : col_start + tile_cols].set(owned[row_start:])
        row_low = (current + 1) * tile_rows
        col_low = (current + 1) * tile_cols
        term = jnp.dot(
            factor_left_rows[row_low:local_rows],
            factor_right_rows.T,
            precision=lax.Precision.HIGHEST,
            preferred_element_type=jnp.float32,
        )
        matrix = matrix.at[row_low:local_rows, col_low:local_cols].add(-term)
    return matrix


def solution(mesh):
    in_specs = (P("row", "col"),)
    out_specs = P("row", "col")
    return jax.shard_map(
        per_device, mesh=mesh, in_specs=in_specs, out_specs=out_specs, check_vma=False
    )
```

profile of v0, /device:TPU:16, one launch (start us, length us, event | category | flops | bytes accessed | tf_op | source)
XLA Modules:
  0.0 630.4 jit_solution(13229825803608452660)
XLA Ops:
  6.5 1.9 copy.35
  9.2 24.6 %all-gather.2 = f32[16,12,512]{2,1,0:T(8,128)S(1)} all-gather(f32[1,12,512]{2,1,0:T(8,128)S(1)} %slice_bitcast_fusion.11), channel_id=1, replica_groups=mesh['row'=32,'col'=16] {'col'}, dimensions={0}, use_global_device_ids=true | all-gather | bytes 417792 | tf_op jit(solution)/shard_map/all_gather | solution.py:55
  34.1 39.3 %all-gather = f32[32,6,12]{2,1,0:T(8,128)S(1)} all-gather(f32[1,6,12]{2,1,0:T(8,128)S(1)} %slice_bitcast_fusion.12), channel_id=1, replica_groups=mesh['row'=32,'col'=16] {'row'}, dimensions={0}, use_global_device_ids=true | all-gather | bytes 9504 | tf_op jit(solution)/shard_map/all_gather | solution.py:49
  73.5 14.9 %all-gather.1 = f32[16,12,192]{2,1,0:T(8,128)S(1)} all-gather(f32[1,12,192]{2,1,0:T(8,128)S(1)} %bitcast.133), channel_id=1, replica_groups=mesh['row'=32,'col'=16] {'col'}, dimensions={0}, use_global_device_ids=true | all-gather | bytes 156672 | tf_op jit(solution)/shard_map/all_gather | solution.py:50
  89.4 11.7 %cholesky.136 = f32[128,128]{1,0:T(8,128)S(1)} custom-call(f32[128,128]{1,0:T(8,128)S(1)} %cholesky.208), custom_call_target="Cholesky" | custom-call | tf_op jit(solution)/shard_map/jit(cholesky)/cholesky | solution.py:52
  101.1 9.8 %custom-call.13 = f32[1,128,128]{1,2,0:T(8,128)S(1)} custom-call(f32[1,128,128]{2,1,0:T(8,128)S(1)} %get-tuple-element.94), custom_call_target="InvertDiagBlocksLowerTriangular" | custom-call | tf_op jit(solution)/shard_map/jit(cholesky)/cholesky | solution.py:52
  111.3 5.8 cholesky.156
  120.7 19.7 %custom-call.14 = f32[2,128,128]{1,2,0:T(8,128)S(1)} custom-call(f32[2,128,128]{2,1,0:T(8,128)S(1)} %pad_maximum_fusion.4), custom_call_target="InvertDiagBlocksLowerTriangular" | custom-call | tf_op jit(solution)/shard_map/triangular_solve/custom-call.0 | solution.py:16
  141.8 1.1 fusion.19
  145.7 153.4 %all-reduce.10.cloned.1.call-done = (f32[512,1,192]{0,2,1:T(8,128)}, f32[512,1,192]{0,2,1:T(8,128)}) async-done(((f32[512,1,192]{0,2,1:T(8,128)}, f32[512,1,192]{0,2,1:T(8,128)}), (f32[512,1,192]{0,2,1:T(8,128)}, f32[512,1,192]{0,2,1:T(8,128)})) %all-reduce.10.cloned.1.call-update) | async-done | bytes 786448 | tf_op jit(solution)/shard_map/psum | solution.py:12
  299.1 1.4 pad_maximum_fusion.1
  300.5 1.3 copy.36
  301.8 1.9 slice.169
  303.8 2.1 slice_add_fusion
  305.8 1.3 copy-done
  307.2 36.3 %all-gather.3 = f32[32,6,12]{2,1,0:T(8,128)S(1)} all-gather(f32[1,6,12]{2,1,0:T(8,128)S(1)} %bitcast.135), channel_id=1, replica_groups=mesh['row'=32,'col'=16] {'row'}, dimensions={0}, use_global_device_ids=true | all-gather | bytes 9504 | tf_op jit(solution)/shard_map/all_gather | solution.py:49
  343.6 18.8 %all-gather.4 = f32[16,12,192]{2,1,0:T(8,128)S(1)} all-gather(f32[1,12,192]{2,1,0:T(8,128)S(1)} %bitcast.134), channel_id=1, replica_groups=mesh['row'=32,'col'=16] {'col'}, dimensions={0}, use_global_device_ids=true | all-gather | bytes 156672 | tf_op jit(solution)/shard_map/all_gather | solution.py:50
  363.4 11.7 %cholesky.174 = f32[128,128]{1,0:T(8,128)S(1)} custom-call(f32[128,128]{1,0:T(8,128)S(1)} %cholesky.211), custom_call_target="Cholesky" | custom-call | tf_op jit(solution)/shard_map/jit(cholesky)/cholesky | solution.py:52
  375.2 9.8 %custom-call.15 = f32[1,128,128]{1,2,0:T(8,128)S(1)} custom-call(f32[1,128,128]{2,1,0:T(8,128)S(1)} %get-tuple-element.92), custom_call_target="InvertDiagBlocksLowerTriangular" | custom-call | tf_op jit(solution)/shard_map/jit(cholesky)/cholesky | solution.py:52
  385.4 5.8 cholesky.194
  394.0 10.9 %scatter-add.6 = f32[512,1024]{0,1:T(8,128)S(1)} dynamic-update-slice(f32[512,1024]{0,1:T(8,128)S(1)} %scatter.6, f32[506,1012]{0,1:T(8,128)} %copy-done, s32[]{:T(128)} %constant.182.clone.1, s32[]{:T(128)} %constant.183.clone.1) | dynamic-update-slice | bytes 4096580 | tf_op jit(solution)/shard_map/scatter-add | solution.py:75
  404.9 16.4 %all-gather.5 = f32[16,12,512]{2,1,0:T(8,128)S(1)} all-gather(f32[1,12,512]{2,1,0:T(8,128)S(1)} %slice_bitcast_fusion.8), channel_id=1, replica_groups=mesh['row'=32,'col'=16] {'col'}, dimensions={0}, use_global_device_ids=true | all-gather | bytes 417792 | tf_op jit(solution)/shard_map/all_gather | solution.py:55
  421.7 19.7 %custom-call.16 = f32[2,128,128]{1,2,0:T(8,128)S(1)} custom-call(f32[2,128,128]{2,1,0:T(8,128)S(1)} %pad_maximum_fusion.5), custom_call_target="InvertDiagBlocksLowerTriangular" | custom-call | tf_op jit(solution)/shard_map/triangular_solve/custom-call.0 | solution.py:16
  442.4 1.0 select_bitcast_fusion.1
  443.6 1.1 scatter.9
  444.7 155.9 %all-reduce.8.cloned.1.call-done = (f32[512,1,192]{0,2,1:T(8,128)}, f32[512,1,192]{0,2,1:T(8,128)}) async-done(((f32[512,1,192]{0,2,1:T(8,128)}, f32[512,1,192]{0,2,1:T(8,128)}), (f32[512,1,192]{0,2,1:T(8,128)}, f32[512,1,192]{0,2,1:T(8,128)})) %all-reduce.8.cloned.1.call-update) | async-done | bytes 786448 | tf_op jit(solution)/shard_map/psum | solution.py:12
  600.6 2.3 pad_maximum_fusion
  602.9 1.9 copy.45
  604.8 1.7 slice.176
  606.5 4.5 slice_add_fusion.1
  611.0 10.8 %scatter-add.9 = f32[512,1024]{0,1:T(8,128)S(1)} dynamic-update-slice(f32[512,1024]{0,1:T(8,128)S(1)} %scatter.9, f32[500,1000]{0,1:T(8,128)} %slice_add_fusion.1, s32[]{:T(128)} %constant.183.clone.1, s32[]{:T(128)} %constant.184.clone.1) | dynamic-update-slice | bytes 4000004 | tf_op jit(solution)/shard_map/scatter-add | solution.py:75
  621.8 1.8 copy.46
  (81 shorter events, 13.4 us)
Async XLA Ops:
  6.5 292.6 %all-reduce.10.cloned.1.call-start = ((), (), s32[]{:S(2)}) async-start(), calls=%async_computation.1 | async-start | bytes 1572864 | tf_op jit(solution)/shard_map/psum | solution.py:12
  120.0 0.6 copy-start.1
  140.4 0.7 copy-start.3
  143.9 456.7 %all-reduce.8.cloned.1.call-start = ((), (), s32[]{:S(2)}) async-start(), calls=%async_computation | async-start | bytes 1572864 | tf_op jit(solution)/shard_map/psum | solution.py:12
  305.8 1.3 copy-start
  404.8 16.7 %copy-start.2 = (f32[128,64]{1,0:T(8,128)S(1)}, f32[128,64]{1,0:T(8,128)}, u32[]{:S(2)}) copy-start(f32[128,64]{1,0:T(8,128)} %copy-done.1) | copy-start | bytes 98308
Sparse Core Ops, SparseCore 0:
  144.0 155.0 all-reduce.9
  443.6 156.9 all-reduce.7
where the time goes:
time: 631 us; the launch traced here: 630 us
  waiting for transfers between devices  309 us (49%)
  blocking collectives  150 us (24%)
  other arithmetic  104 us (16%)
  local copies, waits for them, and re-layouts  39.9 us (6%)
  between operations  16.5 us (3%)
  matrix products  10.2 us (2%)
    psum x2, waiting for transfers between devices, spread(): return lax.psum(block, axis)  309 us
    all_gather x2, blocking collectives, per_device(): corner = lax.all_gather(corner, 'row', axis=0, tiled=True)  75.6 us
    another operation x14, other arithmetic, per_device(): lower_factor = jnp.linalg.cholesky(corner)  57.6 us
    all_gather x2, blocking collectives, per_device(): lax.all_gather(column_block, 'col', axis=1, tiled=True)  41 us
    another operation x10, other arithmetic, solve_rows(): lax.linalg.triangular_solve(lower_factor, rows, left_side=False, lower=Tr...  39.6 us
    all_gather x2, blocking collectives, per_device(): corner = lax.all_gather(corner, 'col', axis=1, tiled=True)  33.6 us
    scatter-add x3, local copies, waits for them, and re-layouts, per_device(): matrix = matrix.at[row_low:local_rows, col_low:local_cols].add(-term)  23.4 us
  transfers between devices with their start and end apart: 2, of which 2 were waited for; matrix products, arithmetic and copies ran while one was open for 0% of the time, Pallas kernels for 0%

commit v1 on v0

--- a/solution.py
+++ b/solution.py
@@ -46,7 +46,9 @@
         corner = matrix[
             factor_row_start : factor_row_start + tile_rows, factor_col_start:factor_col_rest
         ]
-        corner = lax.all_gather(corner, "row", axis=0, tiled=True)
+        corner = jnp.concatenate(
+            lax.all_to_all(jnp.stack([corner] * lax.axis_size("row")), "row", 0, 0), axis=0
+        )
         corner = lax.all_gather(corner, "col", axis=1, tiled=True)
         corner = alternate_cols(alternate_rows(corner, row_count), col_count)
         lower_factor = jnp.linalg.cholesky(corner)

time: 631 us -> 577 us (0.914)
  blocking collectives: 150 us -> 74.9 us
  starting transfers between devices: 0.22 us -> 16.8 us
    all_gather x2 -> x0, blocking collectives: 75.6 us -> none  [per_device(): corner = lax.all_gather(corner, 'row', axis=0, tiled=True)]
    all_to_all x0 -> x2, starting transfers between devices: none -> 16.7 us  [per_device(): lax.all_to_all(jnp.stack([corner] * lax.axis_size('row')), 'row', 0, 0)]
  transfers between devices with their start and end apart: 2 -> 4, of which waited for: 2 -> 2; matrix products, arithmetic and copies ran while one was open for 0% -> 1% of each run, Pallas kernels for 0% -> 0%
where the time goes in v1:
time: 577 us; the launch traced here: 576 us
  waiting for transfers between devices  314 us (54%)
  other arithmetic  105 us (18%)
  blocking collectives  74.9 us (13%)
  local copies, waits for them, and re-layouts  39.9 us (7%)
  starting transfers between devices  16.8 us (3%)
  between operations  16.7 us (3%)
  matrix products  9.39 us (2%)
    psum x2, waiting for transfers between devices, spread(): return lax.psum(block, axis)  314 us
    another operation x14, other arithmetic, per_device(): lower_factor = jnp.linalg.cholesky(corner)  57.6 us
    all_gather x2, blocking collectives, per_device(): lax.all_gather(column_block, 'col', axis=1, tiled=True)  44.1 us
    another operation x10, other arithmetic, solve_rows(): lax.linalg.triangular_solve(lower_factor, rows, left_side=False, lower=Tr...  40.7 us
    all_gather x2, blocking collectives, per_device(): corner = lax.all_gather(corner, 'col', axis=1, tiled=True)  30.8 us
    scatter-add x3, local copies, waits for them, and re-layouts, per_device(): matrix = matrix.at[row_low:local_rows, col_low:local_cols].add(-term)  23.4 us
    all_to_all x2, starting transfers between devices, per_device(): lax.all_to_all(jnp.stack([corner] * lax.axis_size('row')), 'row', 0, 0)  16.7 us
  transfers between devices with their start and end apart: 4, of which 2 were waited for; matrix products, arithmetic and copies ran while one was open for 1% of the time, Pallas kernels for 0%

profile of v1, /device:TPU:16, one launch (start us, length us, event | category | flops | bytes accessed | tf_op | source)
XLA Modules:
  0.0 576.4 jit_solution(11028482352208780487)
XLA Ops:
  7.9 10.1 %all-to-all-start = ((f32[32,6,12]{2,1,0:T(8,128)}), f32[32,6,12]{2,1,0:T(8,128)S(1)}, u32[]{:S(2)}, u32[]{:S(2)}) async-start(f32[32,6,12]{2,1,0:T(8,128)} %stack.16), calls=%async_computation | async-start | bytes 262144 | tf_op jit(solution)/shard_map/all_to_all | solution.py:50
  18.0 1.9 copy.33
  20.0 24.6 %all-gather.1 = f32[16,12,512]{2,1,0:T(8,128)S(1)} all-gather(f32[1,12,512]{2,1,0:T(8,128)S(1)} %slice_bitcast_fusion.11), channel_id=1, replica_groups=mesh['row'=32,'col'=16] {'col'}, dimensions={0}, use_global_device_ids=true | all-gather | bytes 417792 | tf_op jit(solution)/shard_map/all_gather | solution.py:57
  45.6 15.2 %all-gather = f32[16,12,192]{2,1,0:T(8,128)S(1)} all-gather(f32[1,12,192]{2,1,0:T(8,128)S(1)} %bitcast.130), channel_id=1, replica_groups=mesh['row'=32,'col'=16] {'col'}, dimensions={0}, use_global_device_ids=true | all-gather | bytes 156672 | tf_op jit(solution)/shard_map/all_gather | solution.py:52
  61.9 11.7 %cholesky.136 = f32[128,128]{1,0:T(8,128)S(1)} custom-call(f32[128,128]{1,0:T(8,128)S(1)} %cholesky.208), custom_call_target="Cholesky" | custom-call | tf_op jit(solution)/shard_map/jit(cholesky)/cholesky | solution.py:54
  73.6 9.8 %custom-call.13 = f32[1,128,128]{1,2,0:T(8,128)S(1)} custom-call(f32[1,128,128]{2,1,0:T(8,128)S(1)} %get-tuple-element.94), custom_call_target="InvertDiagBlocksLowerTriangular" | custom-call | tf_op jit(solution)/shard_map/jit(cholesky)/cholesky | solution.py:54
  83.8 5.8 %cholesky.156 = f32[64,64]{1,0:T(8,128)S(1)} custom-call(f32[64,64]{1,0:T(8,128)S(1)} %convolution_subtract_fusion.3), custom_call_target="Cholesky" | custom-call | tf_op jit(solution)/shard_map/jit(cholesky)/cholesky | solution.py:54
  92.6 19.9 %custom-call.14 = f32[2,128,128]{1,2,0:T(8,128)S(1)} custom-call(f32[2,128,128]{2,1,0:T(8,128)S(1)} %pad_maximum_fusion.4), custom_call_target="InvertDiagBlocksLowerTriangular" | custom-call | tf_op jit(solution)/shard_map/triangular_solve/custom-call.0 | solution.py:16
  113.5 1.0 select_bitcast_fusion.3
  116.1 155.6 %all-reduce.10.cloned.1.call-done = (f32[512,1,192]{0,2,1:T(8,128)}, f32[512,1,192]{0,2,1:T(8,128)}) async-done(((f32[512,1,192]{0,2,1:T(8,128)}, f32[512,1,192]{0,2,1:T(8,128)}), (f32[512,1,192]{0,2,1:T(8,128)}, f32[512,1,192]{0,2,1:T(8,128)})) %all-reduce.10.cloned.1.call-update) | async-done | bytes 786448 | tf_op jit(solution)/shard_map/psum | solution.py:12
  271.8 1.4 pad_maximum_fusion.1
  273.1 1.3 copy.34
  274.5 1.9 slice.169
  276.4 2.1 slice_add_fusion
  278.5 1.3 copy-done
  279.8 10.8 %scatter-add.6 = f32[512,1024]{0,1:T(8,128)S(1)} dynamic-update-slice(f32[512,1024]{0,1:T(8,128)S(1)} %scatter.6, f32[506,1012]{0,1:T(8,128)} %copy-done, s32[]{:T(128)} %constant.182.clone.1, s32[]{:T(128)} %constant.183.clone.1) | dynamic-update-slice | bytes 4096580 | tf_op jit(solution)/shard_map/scatter-add | solution.py:77
  291.4 6.7 %all-to-all-start.1 = ((f32[32,6,12]{2,1,0:T(8,128)}), f32[32,6,12]{2,1,0:T(8,128)S(1)}, u32[]{:S(2)}, u32[]{:S(2)}) async-start(f32[32,6,12]{2,1,0:T(8,128)} %stack.20), calls=%async_computation.1 | async-start | bytes 262144 | tf_op jit(solution)/shard_map/all_to_all | solution.py:50
  298.1 19.5 %all-gather.3 = f32[16,12,512]{2,1,0:T(8,128)S(1)} all-gather(f32[1,12,512]{2,1,0:T(8,128)S(1)} %slice_bitcast_fusion.8), channel_id=1, replica_groups=mesh['row'=32,'col'=16] {'col'}, dimensions={0}, use_global_device_ids=true | all-gather | bytes 417792 | tf_op jit(solution)/shard_map/all_gather | solution.py:57
  318.1 15.6 %all-gather.2 = f32[16,12,192]{2,1,0:T(8,128)S(1)} all-gather(f32[1,12,192]{2,1,0:T(8,128)S(1)} %bitcast.131), channel_id=1, replica_groups=mesh['row'=32,'col'=16] {'col'}, dimensions={0}, use_global_device_ids=true | all-gather | bytes 156672 | tf_op jit(solution)/shard_map/all_gather | solution.py:52
  334.8 11.7 %cholesky.174 = f32[128,128]{1,0:T(8,128)S(1)} custom-call(f32[128,128]{1,0:T(8,128)S(1)} %cholesky.211), custom_call_target="Cholesky" | custom-call | tf_op jit(solution)/shard_map/jit(cholesky)/cholesky | solution.py:54
  346.5 9.8 %custom-call.15 = f32[1,128,128]{1,2,0:T(8,128)S(1)} custom-call(f32[1,128,128]{2,1,0:T(8,128)S(1)} %get-tuple-element.92), custom_call_target="InvertDiagBlocksLowerTriangular" | custom-call | tf_op jit(solution)/shard_map/jit(cholesky)/cholesky | solution.py:54
  356.7 5.8 %cholesky.194 = f32[64,64]{1,0:T(8,128)S(1)} custom-call(f32[64,64]{1,0:T(8,128)S(1)} %convolution_subtract_fusion.2), custom_call_target="Cholesky" | custom-call | tf_op jit(solution)/shard_map/jit(cholesky)/cholesky | solution.py:54
  365.5 19.9 %custom-call.16 = f32[2,128,128]{1,2,0:T(8,128)S(1)} custom-call(f32[2,128,128]{2,1,0:T(8,128)S(1)} %pad_maximum_fusion.5), custom_call_target="InvertDiagBlocksLowerTriangular" | custom-call | tf_op jit(solution)/shard_map/triangular_solve/custom-call.0 | solution.py:16
  386.5 1.0 select_bitcast_fusion.1
  387.7 1.1 scatter.9
  388.8 157.9 %all-reduce.8.cloned.1.call-done = (f32[512,1,192]{0,2,1:T(8,128)}, f32[512,1,192]{0,2,1:T(8,128)}) async-done(((f32[512,1,192]{0,2,1:T(8,128)}, f32[512,1,192]{0,2,1:T(8,128)}), (f32[512,1,192]{0,2,1:T(8,128)}, f32[512,1,192]{0,2,1:T(8,128)})) %all-reduce.8.cloned.1.call-update) | async-done | bytes 786448 | tf_op jit(solution)/shard_map/psum | solution.py:12
  546.7 2.3 pad_maximum_fusion
  548.9 1.9 copy.43
  550.8 1.7 slice.176
  552.5 4.5 slice_add_fusion.1
  557.0 10.8 %scatter-add.9 = f32[512,1024]{0,1:T(8,128)S(1)} dynamic-update-slice(f32[512,1024]{0,1:T(8,128)S(1)} %scatter.9, f32[500,1000]{0,1:T(8,128)} %slice_add_fusion.1, s32[]{:T(128)} %constant.183.clone.1, s32[]{:T(128)} %constant.184.clone.1) | dynamic-update-slice | bytes 4000004 | tf_op jit(solution)/shard_map/scatter-add | solution.py:77
  567.8 1.8 copy.44
  (83 shorter events, 13.3 us)
Async XLA Ops:
  7.9 37.6 %all-to-all-start = ((f32[32,6,12]{2,1,0:T(8,128)}), f32[32,6,12]{2,1,0:T(8,128)S(1)}, u32[]{:S(2)}, u32[]{:S(2)}) async-start(f32[32,6,12]{2,1,0:T(8,128)} %stack.16), calls=%async_computation | async-start | bytes 262144 | tf_op jit(solution)/shard_map/all_to_all | solution.py:50
  18.0 253.8 %all-reduce.10.cloned.1.call-start = ((), (), s32[]{:S(2)}) async-start(), calls=%async_computation.3 | async-start | bytes 1572864 | tf_op jit(solution)/shard_map/psum | solution.py:12
  61.6 30.9 %copy-start.1 = (f32[128,64]{1,0:T(8,128)S(1)}, f32[128,64]{1,0:T(8,128)}, u32[]{:S(2)}) copy-start(f32[128,64]{1,0:T(8,128)} %pad_convert_fusion) | copy-start | bytes 98308
  278.5 1.3 copy-start
  291.4 26.6 %all-to-all-start.1 = ((f32[32,6,12]{2,1,0:T(8,128)}), f32[32,6,12]{2,1,0:T(8,128)S(1)}, u32[]{:S(2)}, u32[]{:S(2)}) async-start(f32[32,6,12]{2,1,0:T(8,128)} %stack.20), calls=%async_computation.1 | async-start | bytes 262144 | tf_op jit(solution)/shard_map/all_to_all | solution.py:50
  298.1 248.6 %all-reduce.8.cloned.1.call-start = ((), (), s32[]{:S(2)}) async-start(), calls=%async_computation.2 | async-start | bytes 1572864 | tf_op jit(solution)/shard_map/psum | solution.py:12
  334.5 30.9 %copy-start.2 = (f32[128,64]{1,0:T(8,128)S(1)}, f32[128,64]{1,0:T(8,128)}, u32[]{:S(2)}) copy-start(f32[128,64]{1,0:T(8,128)} %pad_convert_fusion) | copy-start | bytes 98308
Sparse Core Ops, SparseCore 0:
  114.7 157.0 all-reduce.9
  387.7 158.9 all-reduce.7
